TPU v7x, 32 devices: a whole 2x2x4 slice. The times are simulated.
32 devices in a mesh: groups: 2 (over y), slab: 4 (over z), pencil: 2 (over x), comp: 2 (over core).
Axes of the slice: x: 2, y: 2, z: 4, core: 2. Of those that a mesh axis runs over, the one named last changes fastest.
Arguments:
- u_start: float32 [3, 64, 64, 512], P(None, ('groups', 'slab'), 'pencil', 'comp'), parts along dimension 1, may hold values from -6 to 6
- toughness: float32 [64, 64, 512], P(('groups', 'slab'), 'pencil', 'comp'), parts along dimension 0, may hold values from 0.3 to 1.5
- crack_label: int32 [64, 64, 512], P(('groups', 'slab'), 'pencil', 'comp'), parts along dimension 0, may hold values from 0 to 2
- obs_weight: bfloat16 [32, 64, 2, 4096], P('slab', 'pencil', 'comp'), may hold values from -0.75 to 0.75
- sensor_cell: int32 [4096], replicated, may hold values from 0 to 4095
Outputs:
- moved: float32 [3, 64, 64, 512], P(None, ('groups', 'slab'), 'pencil', 'comp'), parts along dimension 1
- damage: float32 [64, 64, 512], P(('groups', 'slab'), 'pencil', 'comp'), parts along dimension 0
- readings: float32 [3, 8192], P(None, 'groups'), parts along dimension 1
There are 2 independent parts, one for each index of `groups`. A program takes and returns all parts, laid end to end along the dimension named above; an argument that names none is the same for every part. Nothing has to cross between parts.
Inputs may be any that keep to these rules, and one draw needn't show every extreme that they name: `sensor_cell`: numbers cell blocks as (64 z + y) * 2 + h. `crack_label`: 0 intact, 1 partly cracked, 2 cracked.
All inputs are finite; a program needn't handle non-finite values.
Results may differ from a plain program's by a relative error of at most 0.003.
Values sent between devices are 32-bit elements; how exact they have to be, the bound alone decides.
No kernel may reach another device: no remote copies, remote signals or barrier semaphores. Data moves between devices by JAX's collectives and lax.ppermute only.
A program may use at most 128 MiB of HBM per device.

v0:
```python
import jax
import jax.numpy as jnp
from jax import lax
from jax.sharding import PartitionSpec as P

SHEAR_MODULUS = 1.0
LAME_FIRST = 1.5
RESIDUAL_STIFF = 0.001
TIME_DISP = 0.15
TIME_DAMAGE = 0.08
LENGTH_SCALE = 1.0
DAMAGE_LEVEL = 0.45
POINT_GAIN = 8.0


def with_halo(block, sides, width):
    for axis, dim in sides:
        count = lax.axis_size(axis)
        forward = [(i, i + 1) for i in range(count - 1)]
        backward = [(target, source) for source, target in forward]
        low = lax.ppermute(
            lax.slice_in_dim(block, block.shape[dim] - width, None, axis=dim), axis, forward
        )
        high = lax.ppermute(lax.slice_in_dim(block, 0, width, axis=dim), axis, backward)
        block = jnp.concatenate([low, block, high], axis=dim)
    return block


def central(source, spatial):
    if spatial == 0:
        return 0.5 * (source[..., 2:, 1:-1, 1:-1] - source[..., :-2, 1:-1, 1:-1])
    if spatial == 1:
        return 0.5 * (source[..., 1:-1, 2:, 1:-1] - source[..., 1:-1, :-2, 1:-1])
    return 0.5 * (source[..., 1:-1, 1:-1, 2:] - source[..., 1:-1, 1:-1, :-2])


def shrink(source):
    return source[..., 1:-1, 1:-1, 1:-1]


def laplace(source):
    return (
        source[2:, 1:-1, 1:-1]
        + source[:-2, 1:-1, 1:-1]
        + source[1:-1, 2:, 1:-1]
        + source[1:-1, :-2, 1:-1]
        + source[1:-1, 1:-1, 2:]
        + source[1:-1, 1:-1, :-2]
        - 6.0 * source[1:-1, 1:-1, 1:-1]
    )


def entry_key(first, second):
    return (min(first, second), max(first, second))


def rotate(matrix, first, second):
    other = 3 - first - second
    diag_first = matrix[first, first]
    diag_second = matrix[second, second]
    coupling = matrix[first, second]
    angle = 0.5 * jnp.arctan2(2.0 * coupling, diag_second - diag_first)
    cosine = jnp.cos(angle)
    sine = jnp.sin(angle)
    side_first = matrix[entry_key(other, first)]
    side_second = matrix[entry_key(other, second)]
    result = dict(matrix)
    result[first, first] = (
        cosine * cosine * diag_first - 2.0 * cosine * sine * coupling + sine * sine * diag_second
    )
    result[second, second] = (
        sine * sine * diag_first + 2.0 * cosine * sine * coupling + cosine * cosine * diag_second
    )
    result[first, second] = jnp.zeros_like(coupling)
    result[entry_key(other, first)] = cosine * side_first - sine * side_second
    result[entry_key(other, second)] = sine * side_first + cosine * side_second
    return result


def eigenvalues(matrix):
    for sweep_index in range(5):
        for first, second in ((0, 1), (0, 2), (1, 2)):
            matrix = rotate(matrix, first, second)
    return [matrix[0, 0], matrix[1, 1], matrix[2, 2]]


def advance(padded_disp, padded_damage, toughness):
    gradient = [
        [central(padded_disp[component], direction) for direction in range(3)]
        for component in range(3)
    ]
    strain = {}
    for first in range(3):
        for second in range(first, 3):
            strain[first, second] = 0.5 * (gradient[first][second] + gradient[second][first])
    trace_full = strain[0, 0] + strain[1, 1] + strain[2, 2]
    damage_mid = shrink(padded_damage)
    degrade = (1.0 - damage_mid) ** 2 + RESIDUAL_STIFF
    divergence = []
    for component in range(3):
        total_force = 0.0
        for direction in range(3):
            stress = 2.0 * SHEAR_MODULUS * strain[entry_key(component, direction)]
            if component == direction:
                stress = stress + LAME_FIRST * trace_full
            total_force = total_force + central(degrade * stress, direction)
        divergence.append(total_force)
    moved = shrink(shrink(padded_disp)) + TIME_DISP * jnp.stack(divergence)
    inner = {key_pair: shrink(entry_value) for key_pair, entry_value in strain.items()}
    trace_inner = shrink(trace_full)
    energy = 0.5 * LAME_FIRST * jnp.maximum(trace_inner, 0.0) ** 2
    for eigen_value in eigenvalues(inner):
        energy = energy + SHEAR_MODULUS * jnp.maximum(eigen_value, 0.0) ** 2
    damage_core = shrink(damage_mid)
    damage = damage_core + TIME_DAMAGE * (
        2.0 * (1.0 - damage_core) * energy
        - toughness / LENGTH_SCALE * damage_core
        + toughness * LENGTH_SCALE * laplace(damage_mid)
    )
    return (moved, damage)


def local(u_start, toughness, crack_label, obs_weight, sensor_cell):
    planes, rows, columns = toughness.shape
    damage = DAMAGE_LEVEL * crack_label.astype(jnp.float32)
    moved = u_start
    for repeat in range(2):
        stacked = jnp.concatenate([moved, damage[None]], axis=0)
        padded = with_halo(stacked, (("slab", 1), ("pencil", 2), ("comp", 3)), 2)
        moved, damage = advance(padded[:3], padded[3], toughness)
    pooled = jnp.mean(moved, axis=-1).reshape(3, planes * rows).astype(jnp.bfloat16)
    weight_rows = obs_weight.reshape(planes * rows, obs_weight.shape[-1])
    dense = jnp.dot(pooled, weight_rows, preferred_element_type=jnp.float32)
    plane_ids = lax.axis_index("slab") * planes + jnp.arange(planes, dtype=jnp.int32)
    row_ids = lax.axis_index("pencil") * rows + jnp.arange(rows, dtype=jnp.int32)
    block_ids = (
        (plane_ids[:, None] * (rows * lax.axis_size("pencil")) + row_ids[None, :])
        * lax.axis_size("comp")
        + lax.axis_index("comp")
    ).reshape(planes * rows)
    picks = (block_ids[:, None] == sensor_cell[None, :]).astype(jnp.bfloat16)
    point = jnp.dot(pooled, picks, preferred_element_type=jnp.float32)
    partial_sum = dense + POINT_GAIN * point
    readings = lax.psum(partial_sum, ("slab", "pencil", "comp"))
    return (moved, damage, readings)


def solution(mesh):
    return jax.shard_map(
        local,
        mesh=mesh,
        in_specs=(
            P(None, ("groups", "slab"), "pencil", "comp"),
            P(("groups", "slab"), "pencil", "comp"),
            P(("groups", "slab"), "pencil", "comp"),
            P("slab", "pencil", "comp", None),
            P(),
        ),
        out_specs=(
            P(None, ("groups", "slab"), "pencil", "comp"),
            P(("groups", "slab"), "pencil", "comp"),
            P(None, "groups"),
        ),
        check_vma=False,
    )
```

profile of v0, /device:TPU:0, one launch (start us, length us, event | category | flops | bytes accessed | tf_op | source)
XLA Modules:
  0.0 226.6 jit_solution(18250146474018214217)
XLA Ops:
  2.9 5.0 %collective-permute-start = (f32[4,2,32,256]{3,2,1,0:T(8,128)S(1)}, f32[4,2,32,256]{3,2,1,0:T(8,128)S(1)}, u32[]{:S(2)}, u32[]{:S(2)}) collective-permute-start(f32[4,2,32,256]{3,2,1,0:T(8,128)S(1)} %get-tuple-element.66), channel_id=1, source_target_pairs={{0,4},{4,8},{8,12},{1,5},{5,9},{9,13},{2,6},{6,10},{10,14},{3,7},{... | collective-permute-start | bytes 786440 | tf_op jit(solution)/shard_map/ppermute | solution.py:21
  9.1 4.2 %collective-permute-done = f32[4,2,32,256]{3,2,1,0:T(8,128)S(1)} collective-permute-done((f32[4,2,32,256]{3,2,1,0:T(8,128)S(1)}, f32[4,2,32,256]{3,2,1,0:T(8,128)S(1)}, u32[]{:S(2)}, u32[]{:S(2)}) %collective-permute-start) | collective-permute-done | bytes 262176 | tf_op jit(solution)/shard_map/ppermute | solution.py:21
  13.4 4.1 %collective-permute-done.1 = f32[4,2,32,256]{3,2,1,0:T(8,128)S(1)} collective-permute-done((f32[4,2,32,256]{3,2,1,0:T(8,128)S(1)}, f32[4,2,32,256]{3,2,1,0:T(8,128)S(1)}, u32[]{:S(2)}, u32[]{:S(2)}) %collective-permute-start.1) | collective-permute-done | bytes 262176 | tf_op jit(solution)/shard_map/ppermute | solution.py:24
  18.7 3.4 %collective-permute-start.2 = (f32[4,12,2,256]{3,2,1,0:T(2,128)S(1)}, f32[4,12,2,256]{3,2,1,0:T(2,128)S(1)}, u32[]{:S(2)}, u32[]{:S(2)}) collective-permute-start(f32[4,12,2,256]{3,2,1,0:T(2,128)S(1)} %get-tuple-element.58), channel_id=1, source_target_pairs={{0,2},{1,3},{4,6},{5,7},{8,10},{9,11},{12,14},{13,15},{16,18},{17,... | collective-permute-start | bytes 294920 | tf_op jit(solution)/shard_map/ppermute | solution.py:21
  24.3 4.3 %collective-permute-done.3 = f32[4,12,2,256]{3,2,1,0:T(2,128)S(1)} collective-permute-done((f32[4,12,2,256]{3,2,1,0:T(2,128)S(1)}, f32[4,12,2,256]{3,2,1,0:T(2,128)S(1)}, u32[]{:S(2)}, u32[]{:S(2)}) %collective-permute-start.3) | collective-permute-done | bytes 98336 | tf_op jit(solution)/shard_map/ppermute | solution.py:24
  28.9 1.6 fusion.80
  30.5 1.6 copy.24
  32.2 1.9 collective-permute-start.4
  34.1 2.2 copy.25
  37.6 2.2 copy.26
  39.8 2.2 copy.27
  42.0 3.1 %pad_maximum_fusion = f32[4,12,36,260]{3,2,1,0:T(8,128)S(1)} fusion(f32[4,12,36,2]{3,2,1,0:T(8,128)} %copy.27, f32[4,12,2,256]{3,2,1,0:T(2,128)} %copy-done.13, f32[4,2,32,256]{3,2,1,0:T(8,128)} %copy-done.5, f32[1,8,32,256]{3,2,1,0:T(8,128)S(1)} %multiply_bitcast_fusion, f32[3,8,32,256]{3,2,1,0:T(8,128)S(1)} %copy-done.1, ...), kind=kLoop, calls=%fused_computation.3 | loop fusion | flops 3144960 | bytes 3594240 | tf_op jit(solution)/shard_map/concatenate | solution.py:25
  45.3 2.2 multiply_multiply_fusion.5
  50.1 29.3 %fusion.51 = f32[1,8,32,256]{3,2,1,0:T(8,128)S(1)} fusion(f32[8,32,256]{2,1,0:T(8,128)S(1)} %copy-done.15, f32[12,36,260]{2,1,0:T(8,128)S(1)} %get-tuple-element.37, f32[10,34,258]{2,1,0:T(8,128)S(1)} %get-tuple-element.46, f32[10,34,258]{2,1,0:T(8,128)S(1)} %get-tuple-element.47, f32[10,34,258]{2,1,0:T(8,128)S(1)} %get-tuple-element.29, ...), kind=kLoop, calls=%fused_computation.127 | loop fusion | flops 23068672 | bytes 4194304 | tf_op jit(solution)/shard_map/broadcast_in_dim | solution.py:128
  80.3 3.5 %collective-permute-start.6 = (f32[4,2,32,256]{3,2,1,0:T(8,128)}, f32[4,2,32,256]{3,2,1,0:T(8,128)S(1)}, u32[]{:S(2)}, u32[]{:S(2)}) collective-permute-start(f32[4,2,32,256]{3,2,1,0:T(8,128)} %get-tuple-element.64), channel_id=1, source_target_pairs={{0,4},{4,8},{8,12},{1,5},{5,9},{9,13},{2,6},{6,10},{10,14},{3,7},{... | collective-permute-start | bytes 786440 | tf_op jit(solution)/shard_map/ppermute | solution.py:21
  85.7 4.3 %collective-permute-done.6 = f32[4,2,32,256]{3,2,1,0:T(8,128)S(1)} collective-permute-done((f32[4,2,32,256]{3,2,1,0:T(8,128)}, f32[4,2,32,256]{3,2,1,0:T(8,128)S(1)}, u32[]{:S(2)}, u32[]{:S(2)}) %collective-permute-start.6) | collective-permute-done | bytes 262176 | tf_op jit(solution)/shard_map/ppermute | solution.py:21
  90.0 4.7 %collective-permute-done.7 = f32[4,2,32,256]{3,2,1,0:T(8,128)} collective-permute-done((f32[4,2,32,256]{3,2,1,0:T(8,128)}, f32[4,2,32,256]{3,2,1,0:T(8,128)}, u32[]{:S(2)}, u32[]{:S(2)}) %collective-permute-start.7) | collective-permute-done | bytes 262176 | tf_op jit(solution)/shard_map/ppermute | solution.py:24
  95.9 1.5 collective-permute-start.8
  100.0 4.1 %collective-permute-done.9 = f32[4,12,2,256]{3,2,1,0:T(2,128)S(1)} collective-permute-done((f32[4,12,2,256]{3,2,1,0:T(2,128)S(1)}, f32[4,12,2,256]{3,2,1,0:T(2,128)S(1)}, u32[]{:S(2)}, u32[]{:S(2)}) %collective-permute-start.9) | collective-permute-done | bytes 98336 | tf_op jit(solution)/shard_map/ppermute | solution.py:24
  104.1 1.5 pad_maximum_fusion.3
  105.6 1.6 fusion.79
  107.2 1.6 copy.28
  108.8 1.9 collective-permute-start.10
  110.7 2.2 copy.29
  117.0 2.2 copy.30
  119.2 2.2 copy.31
  121.4 3.3 %pad_maximum_fusion.1 = f32[4,12,36,260]{3,2,1,0:T(8,128)S(1)} fusion(f32[4,12,36,2]{3,2,1,0:T(8,128)} %copy.31, f32[4,12,2,256]{3,2,1,0:T(2,128)} %copy-done.12, f32[4,2,32,256]{3,2,1,0:T(8,128)} %collective-permute-done.7, f32[1,8,32,256]{3,2,1,0:T(8,128)S(1)} %fusion.51, f32[3,8,32,256]{3,2,1,0:T(8,128)} %copy-done.2, ...), kind=kLoop, calls=%fused_computation.4 | loop fusion | flops 3144960 | bytes 3594240 | tf_op jit(solution)/shard_map/concatenate | solution.py:25
  124.9 3.8 %multiply_multiply_fusion.2 = (f32[10,34,258]{2,1,0:T(8,128)S(1)}, f32[10,34,258]{2,1,0:T(8,128)}, f32[10,34,258]{2,1,0:T(8,128)S(1)}, f32[10,34,258]{2,1,0:T(8,...) fusion(f32[12,36,260]{2,1,0:T(8,128)S(1)} %get-tuple-element.33, ...), kind=kLoop, calls=%fused_computation.61 | loop fusion | flops 2456160 | bytes 8421120 | tf_op jit(solution)/shard_map/mul | solution.py:106
  128.7 2.1 multiply_multiply_fusion
  133.6 1.4 fusion
  135.0 60.5 %psum.7 = f32[3,4096]{1,0:T(4,128)} all-reduce(f32[3,4096]{1,0:T(4,128)} %fusion), channel_id=1, replica_groups=mesh['groups'=2,'slab'=4,'pencil'=2,'comp'=2] {'slab','pencil','comp'}, use_global_device_ids=true, to_apply=%region_1.0 | all-reduce | flops 12288 | bytes 98304 | tf_op jit(solution)/shard_map/psum | solution.py:144
  195.5 31.0 %fusion.26 = f32[8,32,256]{2,1,0:T(8,128)} fusion(f32[8,32,256]{2,1,0:T(8,128)} %param.6, f32[12,36,260]{2,1,0:T(8,128)S(1)} %copy-done.4, f32[10,34,258]{2,1,0:T(8,128)S(1)} %get-tuple-element.39, f32[10,34,258]{2,1,0:T(8,128)} %get-tuple-element.40, f32[10,34,258]{2,1,0:T(8,128)} %get-tuple-element.18, f32[10,34,258]{2,1,0:T(8,128)} %get-tuple-element.44, ...), kind=kLoop, calls=%fused_computation.82 | loop fusion | flops 23068672 | bytes 4194304 | tf_op jit(solution)/shard_map/add | solution.py:115
  (66 shorter events, 24.4 us)
Async XLA Ops:
  0.6 132.5 %copy-start = (bf16[8,32,1,4096]{3,1,2,0:T(8,128)(2,1)S(1)}, bf16[8,32,1,4096]{3,1,2,0:T(8,128)(2,1)}, u32[]{:S(2)}) copy-start(bf16[8,32,1,4096]{3,1,2,0:T(8,128)(2,1)} %param.8) | copy-start | bytes 6291460
  0.6 28.0 %copy-start.1 = (f32[3,8,32,256]{3,2,1,0:T(8,128)S(1)}, f32[3,8,32,256]{3,2,1,0:T(8,128)}, u32[]{:S(2)}) copy-start(f32[3,8,32,256]{3,2,1,0:T(8,128)} %param.5) | copy-start | bytes 2359300
  2.9 10.5 %collective-permute-start = (f32[4,2,32,256]{3,2,1,0:T(8,128)S(1)}, f32[4,2,32,256]{3,2,1,0:T(8,128)S(1)}, u32[]{:S(2)}, u32[]{:S(2)}) collective-permute-start(f32[4,2,32,256]{3,2,1,0:T(8,128)S(1)} %get-tuple-element.66), channel_id=1, source_target_pairs={{0,4},{4,8},{8,12},{1,5},{5,9},{9,13},{2,6},{6,10},{10,14},{3,7},{... | collective-permute-start | bytes 786440 | tf_op jit(solution)/shard_map/ppermute | solution.py:21
  7.8 9.7 %collective-permute-start.1 = (f32[4,2,32,256]{3,2,1,0:T(8,128)S(1)}, f32[4,2,32,256]{3,2,1,0:T(8,128)S(1)}, u32[]{:S(2)}, u32[]{:S(2)}) collective-permute-start(f32[4,2,32,256]{3,2,1,0:T(8,128)S(1)} %get-tuple-element.67), channel_id=1, source_target_pairs={{4,0},{8,4},{12,8},{5,1},{9,5},{13,9},{6,2},{10,6},{14,10},{7,3},{... | collective-permute-start | bytes 786440 | tf_op jit(solution)/shard_map/ppermute | solution.py:24
  17.5 13.0 %copy-start.5 = (f32[4,2,32,256]{3,2,1,0:T(8,128)}, f32[4,2,32,256]{3,2,1,0:T(8,128)S(1)}, u32[]{:S(2)}) copy-start(f32[4,2,32,256]{3,2,1,0:T(8,128)S(1)} %collective-permute-done.1) | copy-start | bytes 786436
  18.7 5.6 %collective-permute-start.2 = (f32[4,12,2,256]{3,2,1,0:T(2,128)S(1)}, f32[4,12,2,256]{3,2,1,0:T(2,128)S(1)}, u32[]{:S(2)}, u32[]{:S(2)}) collective-permute-start(f32[4,12,2,256]{3,2,1,0:T(2,128)S(1)} %get-tuple-element.58), channel_id=1, source_target_pairs={{0,2},{1,3},{4,6},{5,7},{8,10},{9,11},{12,14},{13,15},{16,18},{17,... | collective-permute-start | bytes 294920 | tf_op jit(solution)/shard_map/ppermute | solution.py:21
  22.1 6.5 %collective-permute-start.3 = (f32[4,12,2,256]{3,2,1,0:T(2,128)S(1)}, f32[4,12,2,256]{3,2,1,0:T(2,128)S(1)}, u32[]{:S(2)}, u32[]{:S(2)}) collective-permute-start(f32[4,12,2,256]{3,2,1,0:T(2,128)S(1)} %get-tuple-element.59), channel_id=1, source_target_pairs={{2,0},{3,1},{6,4},{7,5},{10,8},{11,9},{14,12},{15,13},{18,16},{19,... | collective-permute-start | bytes 294920 | tf_op jit(solution)/shard_map/ppermute | solution.py:24
  28.6 1.9 copy-start.13
  32.2 5.4 %collective-permute-start.4 = (f32[4,12,36,2]{2,0,3,1:T(4,128)S(1)}, f32[4,12,36,2]{2,0,3,1:T(4,128)}, u32[]{:S(2)}, u32[]{:S(2)}) collective-permute-start(f32[4,12,36,2]{2,0,3,1:T(4,128)S(1)} %copy.24), channel_id=1, source_target_pairs={{0,1},{2,3},{4,5},{6,7},{8,9},{10,11},{12,13},{14,15},{16,17},{18,... | collective-permute-start | bytes 41480 | tf_op jit(solution)/shard_map/ppermute | solution.py:21
  36.3 3.5 %collective-permute-start.5 = (f32[4,12,36,2]{2,0,3,1:T(4,128)}, f32[4,12,36,2]{2,0,3,1:T(4,128)}, u32[]{:S(2)}, u32[]{:S(2)}) collective-permute-start(f32[4,12,36,2]{2,0,3,1:T(4,128)} %copy.25), channel_id=1, source_target_pairs={{1,0},{3,2},{5,4},{7,6},{9,8},{11,10},{13,12},{15,14},{17,16},{19,... | collective-permute-start | bytes 41480 | tf_op jit(solution)/shard_map/ppermute | solution.py:24
  48.8 1.3 copy-start.15
  49.9 29.5 %copy-start.6 = (f32[1,8,32,256]{3,2,1,0:T(8,128)}, f32[1,8,32,256]{3,2,1,0:T(8,128)S(1)}, u32[]{:S(2)}) copy-start(f32[1,8,32,256]{3,2,1,0:T(8,128)S(1)} %get-tuple-element.71) | copy-start | bytes 786436
  49.9 29.5 %copy-start.8 = (f32[1,8,32,256]{3,2,1,0:T(8,128)}, f32[1,8,32,256]{3,2,1,0:T(8,128)S(1)}, u32[]{:S(2)}) copy-start(f32[1,8,32,256]{3,2,1,0:T(8,128)S(1)} %get-tuple-element.72) | copy-start | bytes 786436
  50.0 29.5 %copy-start.10 = (f32[1,8,32,256]{3,2,1,0:T(8,128)}, f32[1,8,32,256]{3,2,1,0:T(8,128)S(1)}, u32[]{:S(2)}) copy-start(f32[1,8,32,256]{3,2,1,0:T(8,128)S(1)} %get-tuple-element.73) | copy-start | bytes 786436
  50.1 30.2 %copy-start.2 = (f32[3,8,32,256]{3,2,1,0:T(8,128)}, f32[3,8,32,256]{3,2,1,0:T(8,128)S(1)}, u32[]{:S(2)}) copy-start(f32[3,8,32,256]{3,2,1,0:T(8,128)S(1)} %fusion.4) | copy-start | bytes 2359300
  80.3 9.7 %collective-permute-start.6 = (f32[4,2,32,256]{3,2,1,0:T(8,128)}, f32[4,2,32,256]{3,2,1,0:T(8,128)S(1)}, u32[]{:S(2)}, u32[]{:S(2)}) collective-permute-start(f32[4,2,32,256]{3,2,1,0:T(8,128)} %get-tuple-element.64), channel_id=1, source_target_pairs={{0,4},{4,8},{8,12},{1,5},{5,9},{9,13},{2,6},{6,10},{10,14},{3,7},{... | collective-permute-start | bytes 786440 | tf_op jit(solution)/shard_map/ppermute | solution.py:21
  83.8 10.9 %collective-permute-start.7 = (f32[4,2,32,256]{3,2,1,0:T(8,128)}, f32[4,2,32,256]{3,2,1,0:T(8,128)}, u32[]{:S(2)}, u32[]{:S(2)}) collective-permute-start(f32[4,2,32,256]{3,2,1,0:T(8,128)} %get-tuple-element.65), channel_id=1, source_target_pairs={{4,0},{8,4},{12,8},{5,1},{9,5},{13,9},{6,2},{10,6},{14,10},{7,3},{... | collective-permute-start | bytes 786440 | tf_op jit(solution)/shard_map/ppermute | solution.py:24
  95.9 4.1 %collective-permute-start.8 = (f32[4,12,2,256]{3,2,1,0:T(2,128)S(1)}, f32[4,12,2,256]{3,2,1,0:T(2,128)S(1)}, u32[]{:S(2)}, u32[]{:S(2)}) collective-permute-start(f32[4,12,2,256]{3,2,1,0:T(2,128)S(1)} %get-tuple-element.56), channel_id=1, source_target_pairs={{0,2},{1,3},{4,6},{5,7},{8,10},{9,11},{12,14},{13,15},{16,18},{17,... | collective-permute-start | bytes 294920 | tf_op jit(solution)/shard_map/ppermute | solution.py:21
  97.4 6.7 %collective-permute-start.9 = (f32[4,12,2,256]{3,2,1,0:T(2,128)S(1)}, f32[4,12,2,256]{3,2,1,0:T(2,128)S(1)}, u32[]{:S(2)}, u32[]{:S(2)}) collective-permute-start(f32[4,12,2,256]{3,2,1,0:T(2,128)S(1)} %get-tuple-element.57), channel_id=1, source_target_pairs={{2,0},{3,1},{6,4},{7,5},{10,8},{11,9},{14,12},{15,13},{18,16},{19,... | collective-permute-start | bytes 294920 | tf_op jit(solution)/shard_map/ppermute | solution.py:24
  104.1 3.1 %copy-start.12 = (f32[4,12,2,256]{3,2,1,0:T(2,128)}, f32[4,12,2,256]{3,2,1,0:T(2,128)S(1)}, u32[]{:S(2)}) copy-start(f32[4,12,2,256]{3,2,1,0:T(2,128)S(1)} %collective-permute-done.9) | copy-start | bytes 294916
  108.8 8.1 %collective-permute-start.10 = (f32[4,12,36,2]{2,0,3,1:T(4,128)S(1)}, f32[4,12,36,2]{2,0,3,1:T(4,128)}, u32[]{:S(2)}, u32[]{:S(2)}) collective-permute-start(f32[4,12,36,2]{2,0,3,1:T(4,128)S(1)} %copy.28), channel_id=1, source_target_pairs={{0,1},{2,3},{4,5},{6,7},{8,9},{10,11},{12,13},{14,15},{16,17},{18,... | collective-permute-start | bytes 41480 | tf_op jit(solution)/shard_map/ppermute | solution.py:21
  113.0 6.2 %collective-permute-start.11 = (f32[4,12,36,2]{2,0,3,1:T(4,128)}, f32[4,12,36,2]{2,0,3,1:T(4,128)}, u32[]{:S(2)}, u32[]{:S(2)}) collective-permute-start(f32[4,12,36,2]{2,0,3,1:T(4,128)} %copy.29), channel_id=1, source_target_pairs={{1,0},{3,2},{5,4},{7,6},{9,8},{11,10},{13,12},{15,14},{17,16},{19,... | collective-permute-start | bytes 41480 | tf_op jit(solution)/shard_map/ppermute | solution.py:24
  124.9 3.8 %copy-start.3 = (f32[12,36,260]{2,1,0:T(8,128)}, f32[12,36,260]{2,1,0:T(8,128)S(1)}, u32[]{:S(2)}) copy-start(f32[12,36,260]{2,1,0:T(8,128)S(1)} %get-tuple-element.33) | copy-start | bytes 1347844
  130.8 1.2 copy-start.7
  130.8 1.2 copy-start.9
  130.8 1.2 copy-start.11
  132.0 1.6 copy-start.14
  132.0 1.6 copy-start.16
  133.1 62.5 %copy-start.4 = (f32[12,36,260]{2,1,0:T(8,128)S(1)}, f32[12,36,260]{2,1,0:T(8,128)}, u32[]{:S(2)}) copy-start(f32[12,36,260]{2,1,0:T(8,128)} %copy-done.3) | copy-start | bytes 1347844
where the time goes:
time: 228 us; the launch traced here: 227 us
  other arithmetic  89.2 us (39%)
  blocking collectives  60.5 us (27%)
  waiting for transfers between devices  27.4 us (12%)
  starting transfers between devices  24.9 us (11%)
  local copies, waits for them, and re-layouts  21.7 us (10%)
    psum x1, blocking collectives, local(): readings = lax.psum(partial_sum, ('slab', 'pencil', 'comp'))  60.5 us
    add x1, other arithmetic, advance(): damage_core + TIME_DAMAGE * (2.0 * (1.0 - damage_core) * energy - toughne...  31 us
    broadcast_in_dim x2, other arithmetic, local(): stacked = jnp.concatenate([moved, damage[None]], axis=0)  30.5 us
    ppermute x6, waiting for transfers between devices, with_halo(): lax.ppermute(lax.slice_in_dim(block, 0, width, axis=dim), axis, backward)  17.3 us
    ppermute x6, starting transfers between devices, with_halo(): lax.ppermute(lax.slice_in_dim(block, block.shape[dim] - width, None, axis...  17.2 us
    ppermute x6, waiting for transfers between devices, with_halo(): lax.ppermute(lax.slice_in_dim(block, block.shape[dim] - width, None, axis...  10.2 us
    mul x4, other arithmetic, advance(): total_force = total_force + central(degrade * stress, direction)  9.3 us
    concatenate x4, other arithmetic, with_halo(): block = jnp.concatenate([low, block, high], axis=dim)  8.23 us
  transfers between devices with their start and end apart: 12, of which 8 were waited for; matrix products, arithmetic and copies ran while one was open for 6% of the time, Pallas kernels for 0%

commit v1 on v0

v1 whole, which is shorter than its diff:
```python
import functools

import jax
import jax.numpy as jnp
from jax import lax
from jax.experimental import pallas as pl
from jax.experimental.pallas import tpu as pltpu
from jax.sharding import PartitionSpec as P

SHEAR_MODULUS = 1.0
LAME_FIRST = 1.5
RESIDUAL_STIFF = 0.001
TIME_DISP = 0.15
TIME_DAMAGE = 0.08
DAMAGE_LEVEL = 0.45
POINT_GAIN = 8.0
LANES = 128
SUB = 8
COS_THIRD = (
    0.5000000037331834,
    0.5773496613984853,
    -0.11109449276880777,
    0.05327935086024303,
    -0.031925412185213546,
    0.01960032102518762,
    -0.010237508432464154,
    0.003654119632233793,
    -0.0006260453394989179,
)
F32 = jnp.float32
VMEM = pl.BlockSpec(memory_space=pltpu.VMEM)


def positive_square_sum(m00, m11, m22, m01, m02, m12):
    mean = (m00 + m11 + m22) * (1.0 / 3.0)
    b00, b11, b22 = m00 - mean, m11 - mean, m22 - mean
    s01, s02, s12 = m01 * m01, m02 * m02, m12 * m12
    p2 = (b00 * b00 + b11 * b11 + b22 * b22) * (1.0 / 6.0) + (s01 + s02 + s12) * (1.0 / 3.0)
    det = b00 * (b11 * b22 - s12) + 2.0 * (m01 * m02) * m12 - b11 * s02 - b22 * s01
    mean2 = mean * mean
    whole = mean * (mean2 - 3.0 * p2) + det
    up = whole >= 0.0
    safe = jnp.maximum(p2, 1e-24)
    inv = lax.rsqrt(safe)
    p = safe * inv
    half = 0.25 * (det * inv) * (inv * inv)
    half = jnp.where(up, half, -half) + 0.5
    half = jnp.minimum(jnp.maximum(half, 0.0), 1.0)
    t = jnp.sqrt(half)
    c = jnp.full_like(t, COS_THIRD[-1])
    for value in COS_THIRD[-2::-1]:
        c = c * t + value
    pc = p * c
    lead = jnp.where(up, mean, -mean)
    largest = lead + 2.0 * pc
    square = largest * largest
    norm = 6.0 * p2 + 3.0 * mean2
    rest = lead - pc
    return jnp.where(
        up, jnp.where(rest > 0.0, norm, square), jnp.where(rest < 0.0, norm - square, 0.0)
    )


def emit_payloads(merged, py, u, d, zup, zdn, ys, dgs):
    _, Z, Y, X = u.shape
    for c in range(3):
        zup[2 * c : 2 * c + 2] = u[c, Z - 2 : Z]
        zdn[2 * c : 2 * c + 2] = u[c, 0:2]
    zup[6] = d[Z - 1]
    zdn[6] = d[0]

    def rows(side, c, layer, zs):
        row = Y - 2 + layer if side > 0 else layer
        return u[c, zs, row, :]

    def pick(fn):
        if merged:
            first = py == 0
            return [jnp.where(first, fn(1), fn(-1))]
        return [fn(1), fn(-1)]

    full = slice(0, Z)
    for c in range(3):
        for layer in range(2):
            for ref, value in zip(ys, pick(lambda s: rows(s, c, layer, full))):
                ref[2 * c + layer] = value
    for ref, value in zip(ys, pick(lambda s: d[:, Y - 1 if s > 0 else 0, :])):
        ref[6] = value
    n = len(ys)
    for k, zs in enumerate((slice(Z - 1, Z), slice(0, 1))):
        for c in range(3):
            for j, value in enumerate(
                pick(lambda s: rows(s, c, 1 if s > 0 else 0, zs))
            ):
                dgs[k * n + j][c : c + 1, :] = value


def payload_shapes(Z, Y, X, n):
    return (
        [jax.ShapeDtypeStruct((7, Y, X), F32)] * 2
        + [jax.ShapeDtypeStruct((7, Z, X), F32)] * n
        + [jax.ShapeDtypeStruct((SUB, X), F32)] * (2 * n)
    )


def pack_kernel(merged, n, u, label, d0, zup, zdn, *rest):
    d0[...] = DAMAGE_LEVEL * label[...].astype(F32)
    emit_payloads(merged, lax.axis_index("pencil"), u, d0, zup, zdn, rest[:n], rest[n:])


def xpack_kernel(merged, u, d, zlo, zhi, ylo, yhi, out):
    _, Z, Y, X = u.shape
    left = lax.axis_index("comp") == 0
    lane = lax.broadcasted_iota(jnp.int32, (Y, LANES), 1)
    slot = jnp.where(left, (lane + 2) // 2 % (LANES // 2), lane // 2)

    def side(ref, *at):
        return jnp.where(left, ref[at + (slice(X - LANES, X),)], ref[at + (slice(0, LANES),)])

    acc = jnp.zeros((Y, LANES), F32)
    entry = 0
    for c in range(3):
        for z in range(-1, Z + 1):
            if z < 0:
                tile = side(zlo, 2 * c + 1, slice(None))
            elif z == Z:
                tile = side(zhi, 2 * c, slice(None))
            else:
                tile = side(u, c, z, slice(None))
            acc = jnp.where(slot == entry, pltpu.roll(tile, 2 * entry, 1), acc)
            entry += 1
    for z in range(Z):
        acc = jnp.where(slot == entry, pltpu.roll(side(d, z, slice(None)), 2 * entry, 1), acc)
        entry += 1
    out[0:Y, :] = jnp.where(left, pltpu.roll(acc, 2, 1), acc)
    acc = jnp.zeros((Z, LANES), F32)
    entry = 0
    for ref, layer in ((ylo, 1), (yhi, 0)):
        for c in range(3):
            tile = side(ref, 2 * c + layer, slice(None))
            acc = jnp.where(slot[0:Z] == entry, pltpu.roll(tile, 2 * entry, 1), acc)
            entry += 1
    out[Y : Y + Z, :] = jnp.where(left, pltpu.roll(acc, 2, 1), acc)


def gather_blocks(merged, refs, U, D):
    u, d, zlo, zhi, ylo, yhi, dgs, xh = refs
    _, Z, Y, X = u.shape
    H = SUB
    py = lax.axis_index("pencil")
    left = lax.axis_index("comp") == 0
    lo_ok = py != 0 if merged else None
    hi_ok = py == 0 if merged else None

    def keep(ok, value):
        return value if ok is None else jnp.where(ok, value, 0.0)

    lane = lax.broadcasted_iota(jnp.int32, (Y, LANES), 1)
    inside = jnp.where(left, lane, LANES - 1 - lane) < 2
    packet = xh[0:Y, :]
    packet = jnp.where(left, packet, pltpu.roll(packet, LANES - 2, 1))
    edge = xh[Y : Y + Z, :]
    edge = jnp.where(left, edge, pltpu.roll(edge, LANES - 2, 1))

    def column(source, entry):
        shift = (LANES - 2 * entry) % LANES
        moved = pltpu.roll(source, shift, 1) if shift else source
        return jnp.where(inside[0 : source.shape[0]], moved, 0.0)

    entry = 0
    for c in range(3):
        U[c, 2 : Z + 2, H : H + Y, 0:X] = u[c]
        U[c, 0:2, H : H + Y, 0:X] = zlo[2 * c : 2 * c + 2]
        U[c, Z + 2 : Z + 4, H : H + Y, 0:X] = zhi[2 * c : 2 * c + 2]
        for z in range(-1, Z + 1):
            U[c, z + 2, H : H + Y, X : X + LANES] = column(packet, entry)
            entry += 1
        for layer in range(2):
            low = keep(lo_ok, ylo[2 * c + layer])
            high = keep(hi_ok, yhi[2 * c + layer])
            for z in range(Z):
                U[c, z + 2, H - 2 + layer : H - 1 + layer, 0:X] = low[z : z + 1]
                U[c, z + 2, H + Y + layer : H + Y + layer + 1, 0:X] = high[z : z + 1]
        low, high = keep(lo_ok, column(edge, c)), keep(hi_ok, column(edge, 3 + c))
        for z in range(Z):
            U[c, z + 2, H - 1 : H, X : X + LANES] = low[z : z + 1]
            U[c, z + 2, H + Y : H + Y + 1, X : X + LANES] = high[z : z + 1]
        n = len(dgs) // 2
        for k, zi in ((0, 1), (1, Z + 2)):
            from_low = dgs[k * n][c : c + 1, :]
            from_high = dgs[k * n + n - 1][c : c + 1, :]
            U[c, zi, H - 1 : H, 0:X] = keep(lo_ok, from_low)
            U[c, zi, H + Y : H + Y + 1, 0:X] = keep(hi_ok, from_high)
    D[1 : Z + 1, H : H + Y, 0:X] = d[...]
    D[0, H : H + Y, 0:X] = zlo[6]
    D[Z + 1, H : H + Y, 0:X] = zhi[6]
    low, high = keep(lo_ok, ylo[6]), keep(hi_ok, yhi[6])
    for z in range(Z):
        D[z + 1, H : H + Y, X : X + LANES] = column(packet, entry)
        D[z + 1, H - 1 : H, 0:X] = low[z : z + 1]
        D[z + 1, H + Y : H + Y + 1, 0:X] = high[z : z + 1]
        entry += 1


def ahead(value):
    return pltpu.roll(value, value.shape[-1] - 1, value.ndim - 1)


def behind(value):
    return pltpu.roll(value, 1, value.ndim - 1)


def step_kernel(merged, n, last, *refs):
    u, d, tough, zlo, zhi = refs[:5]
    rest = list(refs[5:])
    take = lambda k: [rest.pop(0) for _ in range(k)]
    ys, dgs, (xh,) = take(n), take(2 * n), take(1)
    if last:
        weight, sensor = take(2)
    moved, damage = take(2)
    if last:
        (part,) = take(1)
    else:
        zup, zdn, *out = take(2 + 3 * n)
    U, D, S = take(3)
    _, Z, Y, X = u.shape
    H = SUB
    gather_blocks(merged, (u, d, zlo, zhi, ys[0], ys[-1], dgs, xh), U, D)
    zz, zy, zx, yy, yx, xx = range(6)
    tiles = Y // SUB

    def gradients(zi, r):
        at = slice(r, r + SUB)
        gz, gy, gx = [], [], []
        for c in range(3):
            gz.append(U[c, zi + 1, at, :] - U[c, zi - 1, at, :])
            gy.append(U[c, zi, r + 1 : r + SUB + 1, :] - U[c, zi, r - 1 : r + SUB - 1, :])
            mid = U[c, zi, at, :]
            gx.append(ahead(mid) - behind(mid))
        return gz, gy, gx

    def stiffness(zi, r):
        keep = 1.0 - D[zi - 1, r : r + SUB, :]
        return 0.5 * (keep * keep + RESIDUAL_STIFF)

    def put(key, zi, r, value, width):
        S[key, zi - 1, r : r + SUB, 0:width] = value[:, 0:width]

    def z_face(zi):
        for t in range(1, tiles + 1):
            r = t * SUB
            gz, gy, gx = gradients(zi, r)
            h = stiffness(zi, r)
            total = LAME_FIRST * (gz[0] + gy[1] + gx[2])
            put(zz, zi, r, h * (total + 2.0 * gz[0]), X)
            put(zy, zi, r, h * (gy[0] + gz[1]), X)
            put(zx, zi, r, h * (gx[0] + gz[2]), X)

    z_face(1)
    z_face(Z + 2)

    @pl.loop(2, Z + 2)
    def _(zi):
        for t in (0, tiles + 1):
            r = t * SUB
            at = slice(r, r + SUB)
            row = H - 1 if t == 0 else H + Y
            one = slice(row, row + 1)
            gz, gy, gx = [], [], []
            for c in range(3):
                gz.append(U[c, zi + 1, one, :] - U[c, zi - 1, one, :])
                gy.append(U[c, zi, row + 1 : row + 2, :] - U[c, zi, row - 1 : row, :])
                mid = U[c, zi, one, :]
                gx.append(ahead(mid) - behind(mid))
            keep = 1.0 - D[zi - 1, one, :]
            h = 0.5 * (keep * keep + RESIDUAL_STIFF)
            total = LAME_FIRST * (gz[0] + gy[1] + gx[2])
            for key, value in (
                (zy, gy[0] + gz[1]),
                (yy, total + 2.0 * gy[1]),
                (yx, gx[1] + gy[2]),
            ):
                S[key, zi - 1, one, 0:X] = (h * value)[:, 0:X]
        for t in range(1, tiles + 1):
            r = t * SUB
            gz, gy, gx = gradients(zi, r)
            h = stiffness(zi, r)
            trace = gz[0] + gy[1] + gx[2]
            total = LAME_FIRST * trace
            mzy, mzx, myx = gy[0] + gz[1], gx[0] + gz[2], gx[1] + gy[2]
            put(zz, zi, r, h * (total + 2.0 * gz[0]), X)
            put(yy, zi, r, h * (total + 2.0 * gy[1]), X)
            put(zy, zi, r, h * mzy, X)
            put(zx, zi, r, h * mzx, X + LANES)
            put(yx, zi, r, h * myx, X + LANES)
            put(xx, zi, r, h * (total + 2.0 * gx[2]), X + LANES)
            cut = lambda value: value[:, 0:X]
            squares = positive_square_sum(
                cut(gz[0]), cut(gy[1]), cut(gx[2]), 0.5 * cut(mzy), 0.5 * cut(mzx), 0.5 * cut(myx)
            )
            grow = jnp.maximum(cut(trace), 0.0)
            energy = (0.25 * 0.5 * LAME_FIRST) * (grow * grow) + (0.25 * SHEAR_MODULUS) * squares
            at = slice(r, r + SUB)
            mid = D[zi - 1, at, :]
            core = cut(mid)
            lap = (
                D[zi, at, 0:X]
                + D[zi - 2, at, 0:X]
                + D[zi - 1, r + 1 : r + SUB + 1, 0:X]
                + D[zi - 1, r - 1 : r + SUB - 1, 0:X]
                + cut(ahead(mid) + behind(mid))
                - 6.0 * core
            )
            own = slice((t - 1) * SUB, t * SUB)
            tgh = tough[zi - 2, own, :]
            damage[zi - 2, own, :] = core + TIME_DAMAGE * (
                2.0 * (1.0 - core) * energy + tgh * (lap - core)
            )

    pairs = ((zz, zy, zx), (zy, yy, yx), (zx, yx, xx))
    if last:
        pooled = rest[0]

    @pl.loop(2, Z + 2)
    def _(zi):
        for t in range(1, tiles + 1):
            r = t * SUB
            at = slice(r, r + SUB)
            own = slice((t - 1) * SUB, t * SUB)
            sums = []
            for c in range(3):
                kz, ky, kx = pairs[c]
                mid = S[kx, zi - 1, at, :]
                force = (
                    S[kz, zi, at, 0:X]
                    - S[kz, zi - 2, at, 0:X]
                    + S[ky, zi - 1, r + 1 : r + SUB + 1, 0:X]
                    - S[ky, zi - 1, r - 1 : r + SUB - 1, 0:X]
                    + (ahead(mid) - behind(mid))[:, 0:X]
                )
                new = u[c, zi - 2, own, :] + (0.5 * TIME_DISP) * force
                moved[c, zi - 2, own, :] = new
                if last:
                    sums.append(jnp.sum(new, axis=-1, keepdims=True))
            if last:
                lane = lax.broadcasted_iota(jnp.int32, (SUB, LANES), 1)
                value = jnp.where(lane == 0, sums[0], jnp.where(lane == 1, sums[1], sums[2]))
                start = pl.multiple_of((zi - 2) * Y + (t - 1) * SUB, SUB)
                pooled[pl.ds(start, SUB), :] = value

    if last:
        means = (pooled[...] * (1.0 / X)).T[0:SUB].astype(jnp.bfloat16)
        blocks = Z * Y
        count = lax.axis_size("comp")
        spread = Y * lax.axis_size("pencil")
        index = lax.broadcasted_iota(jnp.int32, (blocks, 1), 0)
        plane = lax.axis_index("slab") * Z + index // Y
        row = lax.axis_index("pencil") * Y + index % Y
        ids = (plane * spread + row) * count + lax.axis_index("comp")
        chunk = 8 * LANES
        S8 = lax.broadcasted_iota(jnp.int32, (SUB, LANES), 0)
        for k in range(sensor.shape[1] // chunk):
            cols = slice(k * chunk, (k + 1) * chunk)
            picks = jnp.where(ids == sensor[:, cols], POINT_GAIN, 0.0).astype(jnp.bfloat16)
            value = jnp.dot(means, weight[:, cols], preferred_element_type=F32)
            value = value + jnp.dot(means, picks, preferred_element_type=F32)
            for c in range(3):
                tile = jnp.zeros((SUB, LANES), F32)
                for j in range(8):
                    tile = jnp.where(
                        S8 == j, value[c : c + 1, j * LANES : (j + 1) * LANES], tile
                    )
                part[c, k] = tile
    else:
        emit_payloads(
            merged, lax.axis_index("pencil"), moved, damage, zup, zdn, out[:n], out[n:]
        )


def finish_kernel(count, *refs):
    out = refs[-1]
    total = refs[0][...]
    for ref in refs[1:-1]:
        total = total + ref[...]
    for c in range(3):
        for k in range(total.shape[1]):
            for j in range(SUB):
                start = (k * SUB + j) * LANES
                out[c : c + 1, start : start + LANES] = total[c, k, j : j + 1, :]


def call(kernel, outs, *args, scratch=(), name=None):
    many = isinstance(outs, (list, tuple))
    return pl.pallas_call(
        kernel,
        out_shape=outs,
        in_specs=[VMEM] * len(args),
        out_specs=[VMEM] * len(outs) if many else VMEM,
        scratch_shapes=list(scratch),
        compiler_params=pltpu.CompilerParams(vmem_limit_bytes=48 * 1024 * 1024),
        name=name,
    )(*args)


def up_pairs(count):
    return [(i, i + 1) for i in range(count - 1)]


def down_pairs(count):
    return [(i + 1, i) for i in range(count - 1)]


def exchange(zup, zdn, ys, dgs):
    slabs, pencils = lax.axis_size("slab"), lax.axis_size("pencil")
    n = len(ys)
    zlo = lax.ppermute(zup, "slab", up_pairs(slabs))
    zhi = lax.ppermute(zdn, "slab", down_pairs(slabs))
    swap = up_pairs(pencils) + down_pairs(pencils)
    y_pairs = [swap] if n == 1 else [up_pairs(pencils), down_pairs(pencils)]
    new_ys = [lax.ppermute(y, "pencil", pairs) for y, pairs in zip(ys, y_pairs)]
    new_dgs = []
    for k, z_pairs in enumerate((up_pairs(slabs), down_pairs(slabs))):
        for j, pairs in enumerate(y_pairs):
            joint = [
                (za * pencils + ya, zb * pencils + yb) for za, zb in z_pairs for ya, yb in pairs
            ]
            new_dgs.append(lax.ppermute(dgs[k * n + j], ("slab", "pencil"), joint))
    return zlo, zhi, new_ys, new_dgs


def all_sum(value):
    for axis in ("comp", "pencil"):
        count = lax.axis_size(axis)
        bit = 1
        while bit < count:
            value = value + lax.ppermute(value, axis, [(i, i ^ bit) for i in range(count)])
            bit *= 2
    count = lax.axis_size("slab")
    bit = 1
    while count // bit > 4:
        value = value + lax.ppermute(value, "slab", [(i, i ^ bit) for i in range(count)])
        bit *= 2
    terms = [value]
    for k in range(1, count // bit):
        terms.append(lax.ppermute(value, "slab", [(i, i ^ (k * bit)) for i in range(count)]))
    return terms


def local(u_start, toughness, crack_label, obs_weight, sensor_cell):
    Z, Y, X = toughness.shape
    pencils = lax.axis_size("pencil")
    merged = pencils == 2
    n = 1 if merged else 2
    shape = jax.ShapeDtypeStruct
    field, vector = shape((Z, Y, X), F32), shape((3, Z, Y, X), F32)
    payloads = payload_shapes(Z, Y, X, n)
    swap = [(0, 1), (1, 0)]
    d, *out = call(
        functools.partial(pack_kernel, merged, n),
        [field] + payloads,
        u_start,
        crack_label,
        name="pack",
    )
    moved = u_start
    scratch = [
        pltpu.VMEM((3, Z + 4, Y + 2 * SUB, X + LANES), F32),
        pltpu.VMEM((Z + 2, Y + 2 * SUB, X + LANES), F32),
        pltpu.VMEM((6, Z + 2, Y + 2 * SUB, X + LANES), F32),
    ]
    sensors = sensor_cell.shape[0]
    for repeat in range(2):
        last = repeat == 1
        zlo, zhi, ys, dgs = exchange(out[0], out[1], out[2 : 2 + n], out[2 + n :])
        packet = call(
            functools.partial(xpack_kernel, merged),
            shape((Y + Z, LANES), F32),
            moved,
            d,
            zlo,
            zhi,
            ys[0],
            ys[-1],
            name="xpack",
        )
        xh = lax.ppermute(packet, "comp", swap)
        args = [moved, d, toughness, zlo, zhi, *ys, *dgs, xh]
        if last:
            args += [
                obs_weight.reshape(Z * Y, sensors),
                sensor_cell.reshape(1, sensors),
            ]
            moved, d, part = call(
                functools.partial(step_kernel, merged, n, True),
                [vector, field, shape((3, sensors // (SUB * LANES), SUB, LANES), F32)],
                *args,
                scratch=scratch + [pltpu.VMEM((Z * Y, LANES), F32)],
                name="step2",
            )
        else:
            moved, d, *out = call(
                functools.partial(step_kernel, merged, n, False),
                [vector, field] + payloads,
                *args,
                scratch=scratch,
                name="step1",
            )
    terms = all_sum(part)
    readings = call(
        functools.partial(finish_kernel, len(terms)),
        shape((3, sensors), F32),
        *terms,
        name="finish",
    )
    return moved, d, readings


def solution(mesh):
    return jax.shard_map(
        local,
        mesh=mesh,
        in_specs=(
            P(None, ("groups", "slab"), "pencil", "comp"),
            P(("groups", "slab"), "pencil", "comp"),
            P(("groups", "slab"), "pencil", "comp"),
            P("slab", "pencil", "comp", None),
            P(),
        ),
        out_specs=(
            P(None, ("groups", "slab"), "pencil", "comp"),
            P(("groups", "slab"), "pencil", "comp"),
            P(None, "groups"),
        ),
        check_vma=False,
    )
```

time: 228 us -> 74.4 us (0.33)
  other arithmetic: 89.2 us -> 0.02 us
  blocking collectives: 60.5 us -> 0 us
  local copies, waits for them, and re-layouts: 21.7 us -> 2.09 us
  Pallas kernels: 0 us -> 14.2 us
  starting transfers between devices: 24.9 us -> 28.6 us
    psum x1 -> x0, blocking collectives: 60.5 us -> none  [local(): readings = lax.psum(partial_sum, ('slab', 'pencil', 'comp'))]
    add x4 -> x2, other arithmetic: 33 us -> 0.02 us  [all_sum(): value + lax.ppermute(value, axis, [(i, i ^ bit) for i in range(count)])]
    broadcast_in_dim x2 -> x0, other arithmetic: 30.5 us -> none  [local(): stacked = jnp.concatenate([moved, damage[None]], axis=0)]
    pallas_call x0 -> x6, Pallas kernels: none -> 14.2 us  [call(): pl.pallas_call(kernel, out_shape=outs, in_specs=[VMEM] * len(args), out_s...]
    slice x6 -> x0, local copies, waits for them, and re-layouts: 11 us -> none  [the longest x4 6.5 us: with_halo(): lax.slice_in_dim(block, block.shape[dim] - width, None, axis=dim)]
    mul x5 -> x0, other arithmetic: 9.87 us -> none  [the longest x4 9.3 us: advance(): total_force = total_force + central(degrade * stress, direction)]
    ppermute x4 -> x0, local copies, waits for them, and re-layouts: 8.83 us -> none  [the longest x2 4.43 us: with_halo(): lax.ppermute(lax.slice_in_dim(block, block.shape[dim] - width, None, axis...]
    concatenate x4 -> x0, other arithmetic: 8.23 us -> none  [with_halo(): block = jnp.concatenate([low, block, high], axis=dim)]
  transfers between devices with their start and end apart: 12 -> 17, of which waited for: 8 -> 10; matrix products, arithmetic and copies ran while one was open for 6% -> 0% of each run, Pallas kernels for 0% -> 0%
where the time goes in v1:
time: 74.4 us; the launch traced here: 74 us
  starting transfers between devices  28.6 us (38%)
  waiting for transfers between devices  28.5 us (38%)
  Pallas kernels  14.2 us (19%)
  local copies, waits for them, and re-layouts  2.09 us (3%)
  between operations  0.76 us (1%)
    pallas_call x6, Pallas kernels, call(): pl.pallas_call(kernel, out_shape=outs, in_specs=[VMEM] * len(args), out_s...  14.2 us
    ppermute x4, waiting for transfers between devices, exchange(): new_dgs.append(lax.ppermute(dgs[k * n + j], ('slab', 'pencil'), joint))  10.3 us
    ppermute x4, starting transfers between devices, exchange(): new_dgs.append(lax.ppermute(dgs[k * n + j], ('slab', 'pencil'), joint))  9.3 us
    ppermute x2, starting transfers between devices, exchange(): zlo = lax.ppermute(zup, 'slab', up_pairs(slabs))  8.47 us
    ppermute x2, waiting for transfers between devices, exchange(): new_ys = [lax.ppermute(y, 'pencil', pairs) for y, pairs in zip(ys, y_pairs)]  6.33 us
    ppermute x2, waiting for transfers between devices, exchange(): zhi = lax.ppermute(zdn, 'slab', down_pairs(slabs))  5.91 us
    ppermute x3, starting transfers between devices, all_sum(): lax.ppermute(value, 'slab', [(i, i ^ k * bit) for i in range(count)])  4.45 us
    ppermute x2, waiting for transfers between devices, all_sum(): lax.ppermute(value, axis, [(i, i ^ bit) for i in range(count)])  3.85 us
  transfers between devices with their start and end apart: 17, of which 10 were waited for; matrix products, arithmetic and copies ran while one was open for 0% of the time, Pallas kernels for 0%

profile of v1, /device:TPU:0, one launch (start us, length us, event | category | flops | bytes accessed | tf_op | source)
XLA Modules:
  0.0 74.0 jit_solution(18280072894622294427)
XLA Ops:
  0.6 1.1 %copy-done = f32[3,8,32,256]{3,2,1,0:T(8,128)S(1)} copy-done((f32[3,8,32,256]{3,2,1,0:T(8,128)S(1)}, f32[3,8,32,256]{3,2,1,0:T(8,128)}, u32[]{:S(2)}) %copy-start) | copy-done | bytes 786456
  1.8 0.9 %copy-done.3 = s32[8,32,256]{2,1,0:T(8,128)S(1)} copy-done((s32[8,32,256]{2,1,0:T(8,128)S(1)}, s32[8,32,256]{2,1,0:T(8,128)}, u32[]{:S(2)}) %copy-start.3) | copy-done | bytes 262168
  2.7 0.1 pack.1
  2.8 5.0 %collective-permute-start = (f32[7,32,256]{2,1,0:T(8,128)S(1)}, f32[7,32,256]{2,1,0:T(8,128)S(1)}, u32[]{:S(2)}, u32[]{:S(2)}) collective-permute-start(f32[7,32,256]{2,1,0:T(8,128)S(1)} %get-tuple-element.20), channel_id=1, source_target_pairs={{0,4},{4,8},{8,12},{1,5},{5,9},{9,13},{2,6},{6,10},{10,14},{3,7},{... | collective-permute-start | bytes 688136 | tf_op jit(solution)/shard_map/ppermute | solution.py:416
  7.8 1.3 %collective-permute-start.1 = (f32[7,32,256]{2,1,0:T(8,128)S(1)}, f32[7,32,256]{2,1,0:T(8,128)S(1)}, u32[]{:S(2)}, u32[]{:S(2)}) collective-permute-start(f32[7,32,256]{2,1,0:T(8,128)S(1)} %get-tuple-element.21), channel_id=1, source_target_pairs={{4,0},{8,4},{12,8},{5,1},{9,5},{13,9},{6,2},{10,6},{14,10},{7,3},{... | collective-permute-start | bytes 688136 | tf_op jit(solution)/shard_map/ppermute | solution.py:417
  9.1 1.6 %collective-permute-start.2 = (f32[7,8,256]{2,1,0:T(8,128)S(1)}, f32[7,8,256]{2,1,0:T(8,128)S(1)}, u32[]{:S(2)}, u32[]{:S(2)}) collective-permute-start(f32[7,8,256]{2,1,0:T(8,128)S(1)} %get-tuple-element.22), channel_id=1, source_target_pairs={{0,2},{2,0},{1,3},{3,1},{4,6},{6,4},{5,7},{7,5},{8,10},{10,8},{9,1... | collective-permute-start | bytes 172040 | tf_op jit(solution)/shard_map/ppermute | solution.py:420
  10.6 2.7 %collective-permute-done.2.ylo.yhi.refs_5_ = f32[7,8,256]{2,1,0:T(8,128)S(1)} collective-permute-done((f32[7,8,256]{2,1,0:T(8,128)S(1)}, f32[7,8,256]{2,1,0:T(8,128)S(1)}, u32[]{:S(2)}, u32[]{:S(2)}) %collective-permute-start.2) | collective-permute-done | bytes 57376 | tf_op jit(solution)/shard_map/ppermute | solution.py:420
  13.3 3.4 %collective-permute-done.1.zhi.refs_4_ = f32[7,32,256]{2,1,0:T(8,128)S(1)} collective-permute-done((f32[7,32,256]{2,1,0:T(8,128)S(1)}, f32[7,32,256]{2,1,0:T(8,128)S(1)}, u32[]{:S(2)}, u32[]{:S(2)}) %collective-permute-start.1) | collective-permute-done | bytes 229408 | tf_op jit(solution)/shard_map/ppermute | solution.py:417
  16.7 0.3 xpack.2
  17.1 4.5 %collective-permute-start.3 = (f32[8,256]{1,0:T(8,128)S(1)}, f32[8,256]{1,0:T(8,128)S(1)}, u32[]{:S(2)}, u32[]{:S(2)}) collective-permute-start(f32[8,256]{1,0:T(8,128)S(1)} %get-tuple-element.23), channel_id=1, source_target_pairs={{0,6},{2,4},{4,10},{6,8},{8,14},{10,12},{1,7},{3,5},{5,11},{7,9},{... | collective-permute-start | bytes 24584 | tf_op jit(solution)/shard_map/ppermute | solution.py:427
  21.7 1.3 %collective-permute-start.4 = (f32[8,256]{1,0:T(8,128)S(1)}, f32[8,256]{1,0:T(8,128)S(1)}, u32[]{:S(2)}, u32[]{:S(2)}) collective-permute-start(f32[8,256]{1,0:T(8,128)S(1)} %get-tuple-element.24), channel_id=1, source_target_pairs={{4,2},{6,0},{8,6},{10,4},{12,10},{14,8},{5,3},{7,1},{9,7},{11,5},{... | collective-permute-start | bytes 24584 | tf_op jit(solution)/shard_map/ppermute | solution.py:427
  23.0 5.1 %collective-permute-done.4.refs_7_ = f32[8,256]{1,0:T(8,128)S(1)} collective-permute-done((f32[8,256]{1,0:T(8,128)S(1)}, f32[8,256]{1,0:T(8,128)S(1)}, u32[]{:S(2)}, u32[]{:S(2)}) %collective-permute-start.4) | collective-permute-done | bytes 8224 | tf_op jit(solution)/shard_map/ppermute | solution.py:427
  28.1 4.4 %step1.1 = (f32[3,8,32,256]{3,2,1,0:T(8,128)S(1)}, f32[8,32,256]{2,1,0:T(8,128)S(1)}, f32[7,32,256]{2,1,0:T(8,128)S(1)}, f32[7,32,256]{2,1,0:T(8,128)S(1)}, f32[...) custom-call(f32[3,8,32,256]{3,2,1,0:T(8,128)S(1)} %copy-done, ...), custom_call_target="tpu_custom_call" | custom-call | tf_op jit(solution)/shard_map/step1/pallas_call | solution.py:394
  32.5 3.5 %collective-permute-start.6 = (f32[7,32,256]{2,1,0:T(8,128)S(1)}, f32[7,32,256]{2,1,0:T(8,128)S(1)}, u32[]{:S(2)}, u32[]{:S(2)}) collective-permute-start(f32[7,32,256]{2,1,0:T(8,128)S(1)} %get-tuple-element.27), channel_id=1, source_target_pairs={{0,4},{4,8},{8,12},{1,5},{5,9},{9,13},{2,6},{6,10},{10,14},{3,7},{... | collective-permute-start | bytes 688136 | tf_op jit(solution)/shard_map/ppermute | solution.py:416
  36.0 1.3 %collective-permute-start.7 = (f32[7,32,256]{2,1,0:T(8,128)S(1)}, f32[7,32,256]{2,1,0:T(8,128)S(1)}, u32[]{:S(2)}, u32[]{:S(2)}) collective-permute-start(f32[7,32,256]{2,1,0:T(8,128)S(1)} %get-tuple-element.28), channel_id=1, source_target_pairs={{4,0},{8,4},{12,8},{5,1},{9,5},{13,9},{6,2},{10,6},{14,10},{7,3},{... | collective-permute-start | bytes 688136 | tf_op jit(solution)/shard_map/ppermute | solution.py:417
  37.3 0.6 collective-permute-start.8
  37.9 3.6 %collective-permute-done.8.ylo.yhi.refs_5_ = f32[7,8,256]{2,1,0:T(8,128)S(1)} collective-permute-done((f32[7,8,256]{2,1,0:T(8,128)S(1)}, f32[7,8,256]{2,1,0:T(8,128)S(1)}, u32[]{:S(2)}, u32[]{:S(2)}) %collective-permute-start.8) | collective-permute-done | bytes 57376 | tf_op jit(solution)/shard_map/ppermute | solution.py:420
  41.6 2.5 %collective-permute-done.7.zhi.refs_4_ = f32[7,32,256]{2,1,0:T(8,128)S(1)} collective-permute-done((f32[7,32,256]{2,1,0:T(8,128)S(1)}, f32[7,32,256]{2,1,0:T(8,128)S(1)}, u32[]{:S(2)}, u32[]{:S(2)}) %collective-permute-start.7) | collective-permute-done | bytes 229408 | tf_op jit(solution)/shard_map/ppermute | solution.py:417
  44.1 0.3 xpack.3
  44.4 2.2 %collective-permute-start.9 = (f32[8,256]{1,0:T(8,128)S(1)}, f32[8,256]{1,0:T(8,128)S(1)}, u32[]{:S(2)}, u32[]{:S(2)}) collective-permute-start(f32[8,256]{1,0:T(8,128)S(1)} %get-tuple-element.30), channel_id=1, source_target_pairs={{0,6},{2,4},{4,10},{6,8},{8,14},{10,12},{1,7},{3,5},{5,11},{7,9},{... | collective-permute-start | bytes 24584 | tf_op jit(solution)/shard_map/ppermute | solution.py:427
  46.6 1.3 %collective-permute-start.10 = (f32[8,256]{1,0:T(8,128)S(1)}, f32[8,256]{1,0:T(8,128)S(1)}, u32[]{:S(2)}, u32[]{:S(2)}) collective-permute-start(f32[8,256]{1,0:T(8,128)S(1)} %get-tuple-element.31), channel_id=1, source_target_pairs={{4,2},{6,0},{8,6},{10,4},{12,10},{14,8},{5,3},{7,1},{9,7},{11,5},{... | collective-permute-start | bytes 24584 | tf_op jit(solution)/shard_map/ppermute | solution.py:427
  47.9 5.1 %collective-permute-done.10.refs_7_ = f32[8,256]{1,0:T(8,128)S(1)} collective-permute-done((f32[8,256]{1,0:T(8,128)S(1)}, f32[8,256]{1,0:T(8,128)S(1)}, u32[]{:S(2)}, u32[]{:S(2)}) %collective-permute-start.10) | collective-permute-done | bytes 8224 | tf_op jit(solution)/shard_map/ppermute | solution.py:427
  53.0 8.4 %step2.1 = (f32[3,8,32,256]{3,2,1,0:T(8,128)}, f32[8,32,256]{2,1,0:T(8,128)}, f32[3,4,8,128]{3,2,1,0:T(8,128)S(1)}) custom-call(f32[3,8,32,256]{3,2,1,0:T(8,128)S(1)} %get-tuple-element.25.u.refs_0_, f32[8,32,256]{2,1,0:T(8,128)S(1)} %get-tuple-element.26.d.refs_1_, f32[8,32,256]{2,1,0:T(8,128)S(1)} %copy-done.2, ...), custom_call_target="tpu_custom_call" | custom-call | tf_op jit(solution)/shard_map/step2/pallas_call | solution.py:394
  61.4 1.2 %collective-permute-done.12 = f32[3,4,8,128]{3,2,1,0:T(8,128)S(1)} collective-permute-done((f32[3,4,8,128]{3,2,1,0:T(8,128)S(1)}, f32[3,4,8,128]{3,2,1,0:T(8,128)S(1)}, u32[]{:S(2)}, u32[]{:S(2)}) %collective-permute-start.12) | collective-permute-done | bytes 49184 | tf_op jit(solution)/shard_map/ppermute | solution.py:436
  62.7 1.5 %collective-permute-start.13 = (f32[3,4,8,128]{3,2,1,0:T(8,128)S(1)}, f32[3,4,8,128]{3,2,1,0:T(8,128)S(1)}, u32[]{:S(2)}, u32[]{:S(2)}) collective-permute-start(f32[3,4,8,128]{3,2,1,0:T(8,128)S(1)} %add.6), channel_id=1, source_target_pairs={{0,2},{2,0},{1,3},{3,1},{4,6},{6,4},{5,7},{7,5},{8,10},{10,8},{9,1... | collective-permute-start | bytes 147464 | tf_op jit(solution)/shard_map/ppermute | solution.py:436
  64.2 2.6 %collective-permute-done.13 = f32[3,4,8,128]{3,2,1,0:T(8,128)S(1)} collective-permute-done((f32[3,4,8,128]{3,2,1,0:T(8,128)S(1)}, f32[3,4,8,128]{3,2,1,0:T(8,128)S(1)}, u32[]{:S(2)}, u32[]{:S(2)}) %collective-permute-start.13) | collective-permute-done | bytes 49184 | tf_op jit(solution)/shard_map/ppermute | solution.py:436
  66.9 0.1 collective-permute-start.16
  66.9 1.7 %collective-permute-start.15 = (f32[3,4,8,128]{3,2,1,0:T(8,128)S(1)}, f32[3,4,8,128]{3,2,1,0:T(8,128)S(1)}, u32[]{:S(2)}, u32[]{:S(2)}) collective-permute-start(f32[3,4,8,128]{3,2,1,0:T(8,128)S(1)} %add.7.refs_0_), channel_id=1, source_target_pairs={{0,8},{4,12},{8,0},{12,4},{1,9},{5,13},{9,1},{13,5},{2,10},{6,14},... | collective-permute-start | bytes 147464 | tf_op jit(solution)/shard_map/ppermute | solution.py:445
  68.7 2.6 %collective-permute-start.14 = (f32[3,4,8,128]{3,2,1,0:T(8,128)S(1)}, f32[3,4,8,128]{3,2,1,0:T(8,128)S(1)}, u32[]{:S(2)}, u32[]{:S(2)}) collective-permute-start(f32[3,4,8,128]{3,2,1,0:T(8,128)S(1)} %add.7.refs_0_), channel_id=1, source_target_pairs={{0,4},{4,0},{8,12},{12,8},{1,5},{5,1},{9,13},{13,9},{2,6},{6,2},{1... | collective-permute-start | bytes 147464 | tf_op jit(solution)/shard_map/ppermute | solution.py:445
  71.3 1.5 %collective-permute-done.16.refs_3_ = f32[3,4,8,128]{3,2,1,0:T(8,128)S(1)} collective-permute-done((f32[3,4,8,128]{3,2,1,0:T(8,128)S(1)}, f32[3,4,8,128]{3,2,1,0:T(8,128)S(1)}, u32[]{:S(2)}, u32[]{:S(2)}) %collective-permute-start.16) | collective-permute-done | bytes 49184 | tf_op jit(solution)/shard_map/ppermute | solution.py:445
  72.8 0.5 collective-permute-done.14.refs_1_
  73.4 0.7 finish.1
  (20 shorter events, 0.2 us)
Async XLA Ops:
  0.6 1.1 %copy-start = (f32[3,8,32,256]{3,2,1,0:T(8,128)S(1)}, f32[3,8,32,256]{3,2,1,0:T(8,128)}, u32[]{:S(2)}) copy-start(f32[3,8,32,256]{3,2,1,0:T(8,128)} %refs_0_.1) | copy-start | bytes 2359300
  1.8 0.9 %copy-start.3 = (s32[8,32,256]{2,1,0:T(8,128)S(1)}, s32[8,32,256]{2,1,0:T(8,128)}, u32[]{:S(2)}) copy-start(s32[8,32,256]{2,1,0:T(8,128)} %label.1) | copy-start | bytes 786436
  2.7 25.4 %copy-start.2 = (f32[8,32,256]{2,1,0:T(8,128)S(1)}, f32[8,32,256]{2,1,0:T(8,128)}, u32[]{:S(2)}) copy-start(f32[8,32,256]{2,1,0:T(8,128)} %refs_2_.3) | copy-start | bytes 786436
  2.8 10.5 %collective-permute-start = (f32[7,32,256]{2,1,0:T(8,128)S(1)}, f32[7,32,256]{2,1,0:T(8,128)S(1)}, u32[]{:S(2)}, u32[]{:S(2)}) collective-permute-start(f32[7,32,256]{2,1,0:T(8,128)S(1)} %get-tuple-element.20), channel_id=1, source_target_pairs={{0,4},{4,8},{8,12},{1,5},{5,9},{9,13},{2,6},{6,10},{10,14},{3,7},{... | collective-permute-start | bytes 688136 | tf_op jit(solution)/shard_map/ppermute | solution.py:416
  7.8 9.0 %collective-permute-start.1 = (f32[7,32,256]{2,1,0:T(8,128)S(1)}, f32[7,32,256]{2,1,0:T(8,128)S(1)}, u32[]{:S(2)}, u32[]{:S(2)}) collective-permute-start(f32[7,32,256]{2,1,0:T(8,128)S(1)} %get-tuple-element.21), channel_id=1, source_target_pairs={{4,0},{8,4},{12,8},{5,1},{9,5},{13,9},{6,2},{10,6},{14,10},{7,3},{... | collective-permute-start | bytes 688136 | tf_op jit(solution)/shard_map/ppermute | solution.py:417
  9.1 4.2 %collective-permute-start.2 = (f32[7,8,256]{2,1,0:T(8,128)S(1)}, f32[7,8,256]{2,1,0:T(8,128)S(1)}, u32[]{:S(2)}, u32[]{:S(2)}) collective-permute-start(f32[7,8,256]{2,1,0:T(8,128)S(1)} %get-tuple-element.22), channel_id=1, source_target_pairs={{0,2},{2,0},{1,3},{3,1},{4,6},{6,4},{5,7},{7,5},{8,10},{10,8},{9,1... | collective-permute-start | bytes 172040 | tf_op jit(solution)/shard_map/ppermute | solution.py:420
  17.1 36.0 %copy-start.1 = (bf16[8,32,1,4096]{3,1,2,0:T(8,128)(2,1)S(1)}, bf16[8,32,1,4096]{3,1,2,0:T(8,128)(2,1)}, u32[]{:S(2)}) copy-start(bf16[8,32,1,4096]{3,1,2,0:T(8,128)(2,1)} %param.8) | copy-start | bytes 6291460
  17.1 36.0 %copy-start.4 = (s32[4096]{0:T(1024)S(1)}, s32[4096]{0:T(1024)}, u32[]{:S(2)}) copy-start(s32[4096]{0:T(1024)} %param.9) | copy-start | bytes 49156
  17.1 11.1 %collective-permute-start.5 = (f32[40,128]{1,0:T(8,128)S(1)}, f32[40,128]{1,0:T(8,128)S(1)}, u32[]{:S(2)}, u32[]{:S(2)}) collective-permute-start(f32[40,128]{1,0:T(8,128)S(1)} %xpack.2), channel_id=1, source_target_pairs={{0,1},{1,0},{2,3},{3,2},{4,5},{5,4},{6,7},{7,6},{8,9},{9,8},{10,11... | collective-permute-start | bytes 61448 | tf_op jit(solution)/shard_map/ppermute | solution.py:486
  17.1 5.9 %collective-permute-start.3 = (f32[8,256]{1,0:T(8,128)S(1)}, f32[8,256]{1,0:T(8,128)S(1)}, u32[]{:S(2)}, u32[]{:S(2)}) collective-permute-start(f32[8,256]{1,0:T(8,128)S(1)} %get-tuple-element.23), channel_id=1, source_target_pairs={{0,6},{2,4},{4,10},{6,8},{8,14},{10,12},{1,7},{3,5},{5,11},{7,9},{... | collective-permute-start | bytes 24584 | tf_op jit(solution)/shard_map/ppermute | solution.py:427
  21.7 6.4 %collective-permute-start.4 = (f32[8,256]{1,0:T(8,128)S(1)}, f32[8,256]{1,0:T(8,128)S(1)}, u32[]{:S(2)}, u32[]{:S(2)}) collective-permute-start(f32[8,256]{1,0:T(8,128)S(1)} %get-tuple-element.24), channel_id=1, source_target_pairs={{4,2},{6,0},{8,6},{10,4},{12,10},{14,8},{5,3},{7,1},{9,7},{11,5},{... | collective-permute-start | bytes 24584 | tf_op jit(solution)/shard_map/ppermute | solution.py:427
  32.5 9.1 %collective-permute-start.6 = (f32[7,32,256]{2,1,0:T(8,128)S(1)}, f32[7,32,256]{2,1,0:T(8,128)S(1)}, u32[]{:S(2)}, u32[]{:S(2)}) collective-permute-start(f32[7,32,256]{2,1,0:T(8,128)S(1)} %get-tuple-element.27), channel_id=1, source_target_pairs={{0,4},{4,8},{8,12},{1,5},{5,9},{9,13},{2,6},{6,10},{10,14},{3,7},{... | collective-permute-start | bytes 688136 | tf_op jit(solution)/shard_map/ppermute | solution.py:416
  36.0 8.0 %collective-permute-start.7 = (f32[7,32,256]{2,1,0:T(8,128)S(1)}, f32[7,32,256]{2,1,0:T(8,128)S(1)}, u32[]{:S(2)}, u32[]{:S(2)}) collective-permute-start(f32[7,32,256]{2,1,0:T(8,128)S(1)} %get-tuple-element.28), channel_id=1, source_target_pairs={{4,0},{8,4},{12,8},{5,1},{9,5},{13,9},{6,2},{10,6},{14,10},{7,3},{... | collective-permute-start | bytes 688136 | tf_op jit(solution)/shard_map/ppermute | solution.py:417
  37.3 4.2 %collective-permute-start.8 = (f32[7,8,256]{2,1,0:T(8,128)S(1)}, f32[7,8,256]{2,1,0:T(8,128)S(1)}, u32[]{:S(2)}, u32[]{:S(2)}) collective-permute-start(f32[7,8,256]{2,1,0:T(8,128)S(1)} %get-tuple-element.29), channel_id=1, source_target_pairs={{0,2},{2,0},{1,3},{3,1},{4,6},{6,4},{5,7},{7,5},{8,10},{10,8},{9,1... | collective-permute-start | bytes 172040 | tf_op jit(solution)/shard_map/ppermute | solution.py:420
  44.4 8.7 %collective-permute-start.11 = (f32[40,128]{1,0:T(8,128)S(1)}, f32[40,128]{1,0:T(8,128)S(1)}, u32[]{:S(2)}, u32[]{:S(2)}) collective-permute-start(f32[40,128]{1,0:T(8,128)S(1)} %xpack.3), channel_id=1, source_target_pairs={{0,1},{1,0},{2,3},{3,2},{4,5},{5,4},{6,7},{7,6},{8,9},{9,8},{10,11... | collective-permute-start | bytes 61448 | tf_op jit(solution)/shard_map/ppermute | solution.py:486
  44.4 3.5 %collective-permute-start.9 = (f32[8,256]{1,0:T(8,128)S(1)}, f32[8,256]{1,0:T(8,128)S(1)}, u32[]{:S(2)}, u32[]{:S(2)}) collective-permute-start(f32[8,256]{1,0:T(8,128)S(1)} %get-tuple-element.30), channel_id=1, source_target_pairs={{0,6},{2,4},{4,10},{6,8},{8,14},{10,12},{1,7},{3,5},{5,11},{7,9},{... | collective-permute-start | bytes 24584 | tf_op jit(solution)/shard_map/ppermute | solution.py:427
  46.6 6.4 %collective-permute-start.10 = (f32[8,256]{1,0:T(8,128)S(1)}, f32[8,256]{1,0:T(8,128)S(1)}, u32[]{:S(2)}, u32[]{:S(2)}) collective-permute-start(f32[8,256]{1,0:T(8,128)S(1)} %get-tuple-element.31), channel_id=1, source_target_pairs={{4,2},{6,0},{8,6},{10,4},{12,10},{14,8},{5,3},{7,1},{9,7},{11,5},{... | collective-permute-start | bytes 24584 | tf_op jit(solution)/shard_map/ppermute | solution.py:427
  61.4 1.2 %collective-permute-start.12 = (f32[3,4,8,128]{3,2,1,0:T(8,128)S(1)}, f32[3,4,8,128]{3,2,1,0:T(8,128)S(1)}, u32[]{:S(2)}, u32[]{:S(2)}) collective-permute-start(f32[3,4,8,128]{3,2,1,0:T(8,128)S(1)} %get-tuple-element.34), channel_id=1, source_target_pairs={{0,1},{1,0},{2,3},{3,2},{4,5},{5,4},{6,7},{7,6},{8,9},{9,8},{10,11... | collective-permute-start | bytes 147464 | tf_op jit(solution)/shard_map/ppermute | solution.py:436
  62.7 4.2 %collective-permute-start.13 = (f32[3,4,8,128]{3,2,1,0:T(8,128)S(1)}, f32[3,4,8,128]{3,2,1,0:T(8,128)S(1)}, u32[]{:S(2)}, u32[]{:S(2)}) collective-permute-start(f32[3,4,8,128]{3,2,1,0:T(8,128)S(1)} %add.6), channel_id=1, source_target_pairs={{0,2},{2,0},{1,3},{3,1},{4,6},{6,4},{5,7},{7,5},{8,10},{10,8},{9,1... | collective-permute-start | bytes 147464 | tf_op jit(solution)/shard_map/ppermute | solution.py:436
  66.9 6.0 %collective-permute-start.16 = (f32[3,4,8,128]{3,2,1,0:T(8,128)S(1)}, f32[3,4,8,128]{3,2,1,0:T(8,128)S(1)}, u32[]{:S(2)}, u32[]{:S(2)}) collective-permute-start(f32[3,4,8,128]{3,2,1,0:T(8,128)S(1)} %add.7.refs_0_), channel_id=1, source_target_pairs={{0,12},{4,8},{8,4},{12,0},{1,13},{5,9},{9,5},{13,1},{2,14},{6,10},... | collective-permute-start | bytes 147464 | tf_op jit(solution)/shard_map/ppermute | solution.py:445
  66.9 5.9 %collective-permute-start.15 = (f32[3,4,8,128]{3,2,1,0:T(8,128)S(1)}, f32[3,4,8,128]{3,2,1,0:T(8,128)S(1)}, u32[]{:S(2)}, u32[]{:S(2)}) collective-permute-start(f32[3,4,8,128]{3,2,1,0:T(8,128)S(1)} %add.7.refs_0_), channel_id=1, source_target_pairs={{0,8},{4,12},{8,0},{12,4},{1,9},{5,13},{9,1},{13,5},{2,10},{6,14},... | collective-permute-start | bytes 147464 | tf_op jit(solution)/shard_map/ppermute | solution.py:445
  68.7 4.7 %collective-permute-start.14 = (f32[3,4,8,128]{3,2,1,0:T(8,128)S(1)}, f32[3,4,8,128]{3,2,1,0:T(8,128)S(1)}, u32[]{:S(2)}, u32[]{:S(2)}) collective-permute-start(f32[3,4,8,128]{3,2,1,0:T(8,128)S(1)} %add.7.refs_0_), channel_id=1, source_target_pairs={{0,4},{4,0},{8,12},{12,8},{1,5},{5,1},{9,13},{13,9},{2,6},{6,2},{1... | collective-permute-start | bytes 147464 | tf_op jit(solution)/shard_map/ppermute | solution.py:445
